TPU v7x, 32 devices: a whole 2x2x4 slice. The times are simulated.
32 devices in a mesh: seq: 16 (over z, y, core), head: 2 (over x).
Axes of the slice: x: 2, y: 2, z: 4, core: 2. Of those that a mesh axis runs over, the one named last changes fastest.
Arguments:
- tokens: bfloat16 [16384, 768], P(('seq', 'head')), may hold values from -6 to 6
- w_query: bfloat16 [768, 768], replicated, may hold values from -0.3125 to 0.3125
- w_key: bfloat16 [768, 768], replicated, may hold values from -0.21875 to 0.21875
- w_value: bfloat16 [768, 768], replicated, may hold values from -0.21875 to 0.21875
- w_out: bfloat16 [768, 768], replicated, may hold values from -3.5 to 3.5
- gain_attn: float32 [768], replicated, may hold values from 0.5 to 1.5
- shift_attn: float32 [768], replicated, may hold values from -3 to 3
- w_up: bfloat16 [768, 3072], replicated, may hold values from -0.21875 to 0.21875
- w_down: bfloat16 [3072, 768], replicated, may hold values from -0.109375 to 0.109375
- gain_mlp: float32 [768], replicated, may hold values from 0.5 to 1.5
- shift_mlp: float32 [768], replicated, may hold values from -3 to 3
- cotangent: bfloat16 [16384, 768], P(('seq', 'head')), may hold values from -6 to 6
- lengths: int32 [8], replicated, may hold values from 1 to 64, 256 in all
- seq_order: int32 [8], replicated, may hold values from 0 to 7, each once
- rand_blocks: int32 [256, 3], P('seq'), may hold values from 0 to 65535
Outputs:
- output: bfloat16 [16384, 768], P(('seq', 'head'))
- grad_tokens: float32 [16384, 768], P(('seq', 'head'))
- grad_w_query: float32 [768, 768], P('seq')
- grad_w_key: float32 [768, 768], P('seq')
- grad_w_value: float32 [768, 768], P('seq')
- grad_w_out: float32 [768, 768], P('seq')
- grad_gain_attn: float32 [768], P('seq')
- grad_shift_attn: float32 [768], P('seq')
- grad_w_up: float32 [768, 3072], P('seq')
- grad_w_down: float32 [3072, 768], P('seq')
- grad_gain_mlp: float32 [768], P('seq')
- grad_shift_mlp: float32 [768], P('seq')
Inputs may be any that keep to these rules, and one draw needn't show every extreme that they name: lengths of the 8 sequences in blocks of 64 tokens; they sum to 256 and the longest is exactly 64. `seq_order`: each of 0 to 7 once.
All inputs are finite; a program needn't handle non-finite values.
Results may differ from a plain program's by a relative error of at most 0.017.
Values may be sent and summed in bfloat16 or wider, within the bound.
A program may use at most 320 MiB of HBM per device.

v0:
```python
import jax
import jax.numpy as jnp
from jax import lax
from jax.sharding import PartitionSpec as P

DH = 64
BLK = 64
MAXB = 64
eps_norm = 1e-06


def shifted(value, axis, steps):
    count = lax.axis_size(axis)
    first, last = (max(0, -steps), min(count, count - steps))
    return lax.ppermute(value, axis, [(source, source + steps) for source in range(first, last)])


def block_slots(blocks, rand_rows, lengths, seq_order):
    seq_count = lengths.shape[0]
    seq_ids = jnp.arange(seq_count, dtype=jnp.int32)
    packed = jnp.sum(jnp.where(seq_order[:, None] == seq_ids[None, :], lengths[None, :], 0), axis=1)
    seq_ends = jnp.cumsum(packed)
    starts = seq_ends - packed
    holder = jnp.sum((seq_ends[None, :] <= blocks[:, None]).astype(jnp.int32), axis=1)
    chosen = holder[:, None] == seq_ids[None, :]
    seq_first = jnp.sum(jnp.where(chosen, starts[None, :], 0), axis=1)
    seq_span = jnp.sum(jnp.where(chosen, packed[None, :], 0), axis=1)
    offset = blocks - seq_first
    rand_pos = seq_first[:, None] + jnp.mod(rand_rows, seq_span[:, None])
    fixed_cand = jnp.stack(
        [blocks - 1, blocks, blocks + 1, seq_first, seq_first + seq_span - 1], axis=1
    )
    candidate = jnp.concatenate([fixed_cand, rand_pos], axis=1)
    fixed_live = jnp.stack(
        [offset > 0, offset >= 0, offset < seq_span - 1, offset >= 0, offset >= 0], axis=1
    )
    usable = jnp.concatenate([fixed_live, rand_pos >= 0], axis=1)
    kept_list = []
    for column in range(candidate.shape[1]):
        unique = usable[:, column]
        for earlier in range(column):
            unique = unique & jnp.logical_not(
                kept_list[earlier] & (candidate[:, earlier] == candidate[:, column])
            )
        kept_list.append(unique)
    is_live = jnp.stack(kept_list, axis=1)
    key_blocks = jnp.where(is_live, candidate, blocks[:, None])
    return (key_blocks, is_live)


def norm_forward(values, gain_vec, shift_vec):
    center = values - jnp.mean(values, axis=-1, keepdims=True)
    spread = jnp.mean(center * center, axis=-1, keepdims=True)
    inv_dev = lax.rsqrt(spread + eps_norm)
    x_hat = center * inv_dev
    return (x_hat * gain_vec + shift_vec, x_hat, inv_dev)


def norm_backward(grad_in, x_hat, inv_dev, gain_vec):
    grad_gain = jnp.sum(grad_in * x_hat, axis=0)
    grad_shift = jnp.sum(grad_in, axis=0)
    grad_hat = grad_in * gain_vec
    grad_mean = jnp.mean(grad_hat, axis=-1, keepdims=True)
    grad_proj = jnp.mean(grad_hat * x_hat, axis=-1, keepdims=True)
    return (inv_dev * (grad_hat - grad_mean - x_hat * grad_proj), grad_gain, grad_shift)


def gelu_tanh(values):
    return jax.nn.gelu(values, approximate=True)


def kv_from_below(piece):
    return shifted(piece, "seq", 1)


def kv_from_above(piece):
    return shifted(piece, "seq", -1)


def kv_again_below(piece):
    return shifted(piece, "seq", 1)


def kv_again_above(piece):
    return shifted(piece, "seq", -1)


def fill_cycle(kv_local, cycle_reach, from_below, from_above):
    slot_total = 2 * cycle_reach + 1
    buffer = jnp.zeros((slot_total,) + kv_local.shape, kv_local.dtype)
    buffer = lax.dynamic_update_index_in_dim(buffer, kv_local, cycle_reach, 0)

    def advance(cycle_step, cycle_state):
        below_piece, above_piece, filled = cycle_state
        below_piece = from_below(below_piece)
        above_piece = from_above(above_piece)
        filled = lax.dynamic_update_index_in_dim(
            filled, below_piece, cycle_reach - cycle_step - 1, 0
        )
        filled = lax.dynamic_update_index_in_dim(
            filled, above_piece, cycle_reach + cycle_step + 1, 0
        )
        return (below_piece, above_piece, filled)

    return lax.fori_loop(0, cycle_reach, advance, (kv_local, kv_local, buffer))[2]


def gather_slots(buffer, local_rows, heads_here):
    flat_rows = buffer.reshape(-1, BLK, buffer.shape[-1])
    picked = flat_rows[local_rows]
    split_shape = picked.shape[:3] + (2, heads_here, DH)
    picked = picked.reshape(split_shape)
    return (picked[:, :, :, 0], picked[:, :, :, 1])


def score_blocks(q_blocks, key_rows, is_live, score_scale):
    scores = (
        jnp.einsum("cqhd,cskhd->chqsk", q_blocks, key_rows, preferred_element_type=jnp.float32)
        * score_scale
    )
    scores = jnp.where(is_live[:, None, None, :, None], scores, -1e30)
    return scores.reshape(scores.shape[0], scores.shape[1], scores.shape[2], -1)


def body(
    tokens,
    w_query,
    w_key,
    w_value,
    w_out,
    gain_attn,
    shift_attn,
    w_up,
    w_down,
    gain_mlp,
    shift_mlp,
    cotangent,
    lengths,
    seq_order,
    rand_blocks,
):
    score_scale = DH ** (-0.5)
    queries = jnp.dot(tokens, w_query, preferred_element_type=jnp.float32).astype(jnp.bfloat16)
    key_proj = jnp.dot(tokens, w_key, preferred_element_type=jnp.float32).astype(jnp.bfloat16)
    value_proj = jnp.dot(tokens, w_value, preferred_element_type=jnp.float32).astype(jnp.bfloat16)
    q_local, k_local, v_local = (
        lax.all_to_all(queries, "head", split_axis=1, concat_axis=0, tiled=True),
        lax.all_to_all(key_proj, "head", split_axis=1, concat_axis=0, tiled=True),
        lax.all_to_all(value_proj, "head", split_axis=1, concat_axis=0, tiled=True),
    )
    stretch_rows = q_local.shape[0]
    heads_here = q_local.shape[1] // DH
    stretch_blocks = stretch_rows // BLK
    cycle_reach = MAXB * BLK // stretch_rows
    kv_local = jnp.concatenate([k_local, v_local], axis=1)
    buffer = fill_cycle(kv_local, cycle_reach, kv_from_below, kv_from_above)
    seq_index = lax.axis_index("seq")
    blocks = seq_index * stretch_blocks + jnp.arange(stretch_blocks, dtype=jnp.int32)
    key_blocks, is_live = block_slots(blocks, rand_blocks, lengths, seq_order)
    local_rows = key_blocks - (seq_index - cycle_reach) * stretch_blocks
    slot_count = key_blocks.shape[1]
    q_blocks = q_local.reshape(stretch_blocks, BLK, heads_here, DH)
    key_rows, value_rows = gather_slots(buffer, local_rows, heads_here)
    scores = score_blocks(q_blocks, key_rows, is_live, score_scale)
    row_max = jnp.max(scores, axis=-1, keepdims=True)
    exp_scores = jnp.exp(scores - row_max)
    row_total = jnp.sum(exp_scores, axis=-1, keepdims=True)
    attn_probs = exp_scores / row_total
    log_total = row_max + jnp.log(row_total)
    five_shape = (stretch_blocks, heads_here, BLK, slot_count, BLK)
    weights = attn_probs.astype(jnp.bfloat16).reshape(five_shape)
    context = jnp.einsum(
        "chqsk,cskhd->cqhd", weights, value_rows, preferred_element_type=jnp.float32
    )
    context = context.astype(jnp.bfloat16).reshape(stretch_rows, -1)
    context_tok = lax.all_to_all(context, "head", split_axis=0, concat_axis=1, tiled=True)
    attn_out = jnp.dot(context_tok, w_out, preferred_element_type=jnp.float32)
    normed, hat_one, dev_one = norm_forward(
        tokens.astype(jnp.float32) + attn_out, gain_attn, shift_attn
    )
    normed_low = normed.astype(jnp.bfloat16)
    hidden_pre = jnp.dot(normed_low, w_up, preferred_element_type=jnp.float32)
    hidden = gelu_tanh(hidden_pre).astype(jnp.bfloat16)
    mlp_out = jnp.dot(hidden, w_down, preferred_element_type=jnp.float32)
    output, hat_two, dev_two = norm_forward(normed + mlp_out, gain_mlp, shift_mlp)
    grad_two, grad_gain_mlp, grad_shift_mlp = norm_backward(
        cotangent.astype(jnp.float32), hat_two, dev_two, gain_mlp
    )
    grad_mlp = grad_two.astype(jnp.bfloat16)
    grad_w_down = jnp.dot(hidden.T, grad_mlp, preferred_element_type=jnp.float32)
    grad_hidden = jnp.dot(grad_mlp, w_down.T, preferred_element_type=jnp.float32)
    gelu_out, gelu_pull = jax.vjp(gelu_tanh, hidden_pre)
    grad_pre = gelu_pull(grad_hidden)[0].astype(jnp.bfloat16)
    grad_w_up = jnp.dot(normed_low.T, grad_pre, preferred_element_type=jnp.float32)
    grad_normed = grad_two + jnp.dot(grad_pre, w_up.T, preferred_element_type=jnp.float32)
    grad_one, grad_gain_attn, grad_shift_attn = norm_backward(
        grad_normed, hat_one, dev_one, gain_attn
    )
    grad_attn = grad_one.astype(jnp.bfloat16)
    grad_w_out = jnp.dot(context_tok.T, grad_attn, preferred_element_type=jnp.float32)
    grad_context = jnp.dot(grad_attn, w_out.T, preferred_element_type=jnp.float32).astype(
        jnp.bfloat16
    )
    grad_ctx_local = lax.all_to_all(grad_context, "head", split_axis=1, concat_axis=0, tiled=True)
    buffer_back = fill_cycle(kv_local, cycle_reach, kv_again_below, kv_again_above)
    key_again, value_again = gather_slots(buffer_back, local_rows, heads_here)
    scores_again = score_blocks(q_blocks, key_again, is_live, score_scale)
    probs_again = jnp.exp(scores_again - log_total)
    weights_again = probs_again.astype(jnp.bfloat16).reshape(five_shape)
    grad_blocks = grad_ctx_local.reshape(stretch_blocks, BLK, heads_here, DH)
    grad_probs = jnp.einsum(
        "cqhd,cskhd->chqsk", grad_blocks, value_again, preferred_element_type=jnp.float32
    )
    grad_probs = grad_probs.reshape(probs_again.shape)
    grad_value_rows = jnp.einsum(
        "chqsk,cqhd->cskhd", weights_again, grad_blocks, preferred_element_type=jnp.float32
    )
    row_inner = jnp.sum(probs_again * grad_probs, axis=-1, keepdims=True)
    grad_scores = (probs_again * (grad_probs - row_inner)).astype(jnp.bfloat16).reshape(five_shape)
    grad_query = (
        jnp.einsum("chqsk,cskhd->cqhd", grad_scores, key_again, preferred_element_type=jnp.float32)
        * score_scale
    )
    grad_key_rows = (
        jnp.einsum("chqsk,cqhd->cskhd", grad_scores, q_blocks, preferred_element_type=jnp.float32)
        * score_scale
    )
    slot_grads = jnp.concatenate(
        [
            grad_key_rows.reshape(stretch_blocks, slot_count, BLK, -1),
            grad_value_rows.reshape(stretch_blocks, slot_count, BLK, -1),
        ],
        axis=-1,
    )
    width_kv = slot_grads.shape[-1]
    grad_buffer = jnp.zeros((buffer.shape[0] * stretch_blocks, BLK, width_kv), jnp.float32)
    grad_buffer = grad_buffer.at[local_rows.reshape(-1)].add(slot_grads.reshape(-1, BLK, width_kv))
    grad_buffer = grad_buffer.reshape(buffer.shape[0], stretch_rows, width_kv)

    def carry_back(cycle_step, cycle_state):
        below_acc, above_acc = cycle_state
        below_term = lax.dynamic_index_in_dim(grad_buffer, cycle_step, 0, keepdims=False)
        above_term = lax.dynamic_index_in_dim(
            grad_buffer, 2 * cycle_reach - cycle_step, 0, keepdims=False
        )
        below_acc = shifted((below_acc + below_term).astype(jnp.bfloat16), "seq", -1).astype(
            jnp.float32
        )
        above_acc = shifted((above_acc + above_term).astype(jnp.bfloat16), "seq", 1).astype(
            jnp.float32
        )
        return (below_acc, above_acc)

    zero_rows = jnp.zeros((stretch_rows, width_kv), jnp.float32)
    below_acc, above_acc = lax.fori_loop(0, cycle_reach, carry_back, (zero_rows, zero_rows))
    grad_kv = below_acc + above_acc + grad_buffer[cycle_reach]
    half_width = width_kv // 2
    grad_key_local = grad_kv[:, :half_width].astype(jnp.bfloat16)
    grad_value_local = grad_kv[:, half_width:].astype(jnp.bfloat16)
    grad_query_local = grad_query.reshape(stretch_rows, -1).astype(jnp.bfloat16)
    grad_q_tok, grad_k_tok, grad_v_tok = (
        lax.all_to_all(grad_query_local, "head", split_axis=0, concat_axis=1, tiled=True),
        lax.all_to_all(grad_key_local, "head", split_axis=0, concat_axis=1, tiled=True),
        lax.all_to_all(grad_value_local, "head", split_axis=0, concat_axis=1, tiled=True),
    )
    grad_w_query = jnp.dot(tokens.T, grad_q_tok, preferred_element_type=jnp.float32)
    grad_w_key = jnp.dot(tokens.T, grad_k_tok, preferred_element_type=jnp.float32)
    grad_w_value = jnp.dot(tokens.T, grad_v_tok, preferred_element_type=jnp.float32)
    grad_tokens = grad_one + jnp.dot(grad_q_tok, w_query.T, preferred_element_type=jnp.float32)
    grad_tokens = grad_tokens + jnp.dot(grad_k_tok, w_key.T, preferred_element_type=jnp.float32)
    grad_tokens = grad_tokens + jnp.dot(grad_v_tok, w_value.T, preferred_element_type=jnp.float32)
    grad_terms = (
        grad_w_query,
        grad_w_key,
        grad_w_value,
        grad_w_out,
        grad_gain_attn,
        grad_shift_attn,
        grad_w_up,
        grad_w_down,
        grad_gain_mlp,
        grad_shift_mlp,
    )
    shares = (
        lax.psum_scatter(grad_terms[0], "seq", scatter_dimension=0, tiled=True),
        lax.psum_scatter(grad_terms[1], "seq", scatter_dimension=0, tiled=True),
        lax.psum_scatter(grad_terms[2], "seq", scatter_dimension=0, tiled=True),
        lax.psum_scatter(grad_terms[3], "seq", scatter_dimension=0, tiled=True),
        lax.psum_scatter(grad_terms[4], "seq", scatter_dimension=0, tiled=True),
        lax.psum_scatter(grad_terms[5], "seq", scatter_dimension=0, tiled=True),
        lax.psum_scatter(grad_terms[6], "seq", scatter_dimension=0, tiled=True),
        lax.psum_scatter(grad_terms[7], "seq", scatter_dimension=0, tiled=True),
        lax.psum_scatter(grad_terms[8], "seq", scatter_dimension=0, tiled=True),
        lax.psum_scatter(grad_terms[9], "seq", scatter_dimension=0, tiled=True),
    )
    totals = (
        lax.psum(shares[0].astype(jnp.bfloat16), "head").astype(jnp.float32),
        lax.psum(shares[1].astype(jnp.bfloat16), "head").astype(jnp.float32),
        lax.psum(shares[2].astype(jnp.bfloat16), "head").astype(jnp.float32),
        lax.psum(shares[3].astype(jnp.bfloat16), "head").astype(jnp.float32),
        lax.psum(shares[4].astype(jnp.bfloat16), "head").astype(jnp.float32),
        lax.psum(shares[5].astype(jnp.bfloat16), "head").astype(jnp.float32),
        lax.psum(shares[6].astype(jnp.bfloat16), "head").astype(jnp.float32),
        lax.psum(shares[7].astype(jnp.bfloat16), "head").astype(jnp.float32),
        lax.psum(shares[8].astype(jnp.bfloat16), "head").astype(jnp.float32),
        lax.psum(shares[9].astype(jnp.bfloat16), "head").astype(jnp.float32),
    )
    return (
        output.astype(jnp.bfloat16),
        grad_tokens,
        totals[0],
        totals[1],
        totals[2],
        totals[3],
        totals[4],
        totals[5],
        totals[6],
        totals[7],
        totals[8],
        totals[9],
    )


def solution(mesh):
    return jax.shard_map(
        body,
        mesh=mesh,
        in_specs=(
            P(("seq", "head"), None),
            P(),
            P(),
            P(),
            P(),
            P(),
            P(),
            P(),
            P(),
            P(),
            P(),
            P(("seq", "head"), None),
            P(),
            P(),
            P("seq", None),
        ),
        out_specs=(
            P(("seq", "head"), None),
            P(("seq", "head"), None),
            P("seq", None),
            P("seq", None),
            P("seq", None),
            P("seq", None),
            P("seq"),
            P("seq"),
            P("seq", None),
            P("seq", None),
            P("seq"),
            P("seq"),
        ),
        check_vma=False,
    )
```

profile of v0, /device:TPU:0, one launch (start us, length us, event | category | flops | bytes accessed | tf_op | source)
XLA Modules:
  0.0 1420.9 jit_solution(9601776251737171842)
XLA Ops:
  34.3 6.3 all-to-all-done.1
  48.9 5.9 dynamic_update_slice.22
  54.8 138.4 %while.42 = (s32[]{:T(128)}, bf16[1024,768]{1,0:T(8,128)(2,1)}, bf16[1024,768]{1,0:T(8,128)(2,1)}, bf16[9,1024,768]{2,1,0:T(8,128)(2,1)}, s32[]{:T(128)}, /*inde...) while((s32[]{:T(128)}, bf16[1024,768]{1,0:T(8,128)(2,1)}, bf16[1024,768]{1,0:T(8,128)(2,1)}, ...), condition=%wide.region_1.2_spmd, body=%wide.region_0.1_spmd.sunk | while | flops 10 | bytes 25166100 | solution.py:105
  70.0 32.5 %collective-permute-start = (bf16[1024,768]{1,0:T(8,128)(2,1)}, bf16[1024,768]{1,0:T(8,128)(2,1)S(1)}, u32[]{:S(2)}, u32[]{:S(2)}) collective-permute-start(bf16[1024,768]{1,0:T(8,128)(2,1)} %get-tuple-element.438), channel_id=1, source_target_pairs={{0,2},{2,4},{4,6},{6,8},{8,10},{10,12},{12,14},{14,16},{16,18},{18... | collective-permute-start | bytes 4718600 | tf_op jit(solution)/shard_map/while/body/eval_jaxpr/ppermute | solution.py:15
  116.6 18.9 %collective-permute-start = (bf16[1024,768]{1,0:T(8,128)(2,1)}, bf16[1024,768]{1,0:T(8,128)(2,1)S(1)}, u32[]{:S(2)}, u32[]{:S(2)}) collective-permute-start(bf16[1024,768]{1,0:T(8,128)(2,1)} %get-tuple-element.438), channel_id=1, source_target_pairs={{0,2},{2,4},{4,6},{6,8},{8,10},{10,12},{12,14},{14,16},{16,18},{18... | collective-permute-start | bytes 4718600 | tf_op jit(solution)/shard_map/while/body/eval_jaxpr/ppermute | solution.py:15
  147.8 33.1 %collective-permute-start = (bf16[1024,768]{1,0:T(8,128)(2,1)}, bf16[1024,768]{1,0:T(8,128)(2,1)S(1)}, u32[]{:S(2)}, u32[]{:S(2)}) collective-permute-start(bf16[1024,768]{1,0:T(8,128)(2,1)} %get-tuple-element.438), channel_id=1, source_target_pairs={{0,2},{2,4},{4,6},{6,8},{8,10},{10,12},{12,14},{14,16},{16,18},{18... | collective-permute-start | bytes 4718600 | tf_op jit(solution)/shard_map/while/body/eval_jaxpr/ppermute | solution.py:15
  193.2 13.2 gather_fusion
  206.5 38.9 %reshape.689 = bf16[16,8,64,2,6,64]{5,4,3,2,1,0:T(8,128)(2,1)} reshape(bf16[128,64,768]{2,1,0:T(8,128)(2,1)} %gather_fusion) | data formatting | bytes 25165824 | tf_op jit(solution)/shard_map/reshape | solution.py:112
  245.4 28.4 %slice_bitcast_fusion = (bf16[16,8,64,6,64]{4,3,2,1,0:T(8,128)(2,1)}, bf16[16,8,64,1,6,64]{5,4,3,2,1,0:T(8,128)(2,1)}, bf16[16,8,64,1,6,64]{5,4,3,2,1,0:T(8,128)(2,1)}) fusion(bf16[16,8,64,2,6,64]{5,4,3,2,1,0:T(8,128)(2,1)} %reshape.689), kind=kLoop, calls=%fused_computation.149 | loop fusion | bytes 31457280 | tf_op jit(solution)/shard_map/squeeze | solution.py:113
  273.8 11.3 copy.222
  288.0 22.2 %copy.221 = bf16[16,8,64,1,6,64]{2,5,1,4,0,3:T(8,128)(2,1)} copy(bf16[16,8,64,1,6,64]{5,4,3,2,1,0:T(8,128)(2,1)} %get-tuple-element.343) | data formatting | bytes 12582912
  310.2 13.3 fusion.11
  323.5 11.9 fusion.2
  335.4 16.8 %fusion.44 = bf16[16,64,6,64]{1,3,2,0:T(8,128)(2,1)S(1)} fusion(f32[16,6,64]{2,1,0:T(8,128)S(1)} %fusion.2, f32[16,6,64]{2,1,0:T(8,128)S(1)} %get-tuple-element.360, f32[16,6,64,8,64]{2,4,3,1,0:T(8,128)} %bitcast.270, pred[16,8]{1,0:T(8,128)(4,1)S(1)} %copy.170, bf16[16,8,64,1,6,64]{2,5,1,4,0,3:T(8,128)(2,1)} %copy.221), kind=kOutput, calls=%fused_computation.71 | convolution fusion | flops 418775040 | bytes 19710080 | tf_op jit(solution)/shard_map/chqsk,cskhd->cqhd/dot_general | solution.py:172
  361.2 7.2 all-to-all-done.3
  369.7 5.4 fusion.72
  381.8 8.1 fusion.21
  402.0 11.5 copy.181
  417.6 24.2 %multiply_reduce_fusion = (f32[16,6,64]{2,1,0:T(8,128)S(1)}, f32[16,6,64,512]{2,3,1,0}) fusion(f32[16,6,64]{2,1,0:T(8,128)S(1)} %log_add_fusion, pred[16,8]{1,0:T(8,128)(4,1)S(1)} %copy.170, f32[16,6,64,512]{2,3,1,0} %get-tuple-element.361, bf16[16,6,64,512]{2,3,1,0:T(8,128)(2,1)} %bitcast.275, bf16[16,64,6,64]{1,0,3,2:T(8,128)(2,1)S(1)} %reshape.691), kind=kOutput, calls=%fused_computation.11 | convolution fusion | flops 418375680 | bytes 32292992
  441.7 21.7 %multiply_convert_fusion = bf16[16,6,64,8,64]{2,4,3,1,0:T(8,128)(2,1)} fusion(f32[16,6,64]{2,1,0:T(8,128)S(1)} %get-tuple-element.367, f32[16,6,64]{2,1,0:T(8,128)S(1)} %log_add_fusion, pred[16,8]{1,0:T(8,128)(4,1)S(1)} %copy.170, f32[16,6,64,512]{2,3,1,0} %get-tuple-element.368, f32[16,6,64,512]{2,3,1,0} %get-tuple-element.361), kind=kLoop, calls=%fused_computation.10 | loop fusion | flops 18874368 | bytes 31506560 | tf_op jit(solution)/shard_map/convert_element_type | solution.py:219
  463.4 10.7 fusion.41
  484.0 25.2 %fusion.12 = f32[16,8,64,6,64]{2,4,1,3,0:T(8,128)} fusion(f32[16,6,64]{2,1,0:T(8,128)S(1)} %log_add_fusion, f32[16,6,64,8,64]{2,4,3,1,0:T(8,128)} %bitcast.271, pred[16,8]{1,0:T(8,128)(4,1)S(1)} %copy.170, bf16[16,64,6,64,1]{1,0,3,2,4:T(8,128)(2,1)S(1)} %bitcast.277), kind=kOutput, calls=%fused_computation.27 | convolution fusion | flops 415236096 | bytes 25976960 | tf_op jit(solution)/shard_map/chqsk,cqhd->cskhd/dot_general | solution.py:215
  509.1 13.0 multiply_bitcast_fusion
  522.1 29.1 %copy.190 = f32[16,8,64,6,64]{4,3,2,1,0:T(8,128)} copy(f32[16,8,64,6,64]{4,2,1,3,0:T(8,128)} %multiply_bitcast_fusion) | data formatting | bytes 25165824 | tf_op jit(solution)/shard_map/mul | solution.py:225
  551.2 25.1 %concatenate.51 = f32[128,64,384]{2,1,0:T(8,128)} reshape(f32[16,8,64,6,64]{4,3,2,1,0:T(8,128)} %copy.190) | data formatting | bytes 25165824 | tf_op jit(solution)/shard_map/concatenate | solution.py:228
  576.3 28.8 %copy.193 = f32[16,8,64,6,64]{4,3,2,1,0:T(8,128)} copy(f32[16,8,64,6,64]{2,4,1,3,0:T(8,128)} %fusion.12) | data formatting | bytes 25165824 | tf_op jit(solution)/shard_map/chqsk,cqhd->cskhd/transpose | solution.py:215
  605.1 25.2 %concatenate.52 = f32[128,64,384]{2,1,0:T(8,128)} reshape(f32[16,8,64,6,64]{4,3,2,1,0:T(8,128)} %copy.193) | data formatting | bytes 25165824 | tf_op jit(solution)/shard_map/concatenate | solution.py:228
  635.1 17.4 %pad_maximum_fusion = f32[128,64,768]{2,1,0:T(8,128)} fusion(f32[128,64,384]{2,1,0:T(8,128)} %concatenate.52, f32[128,64,384]{2,1,0:T(8,128)} %concatenate.51), kind=kLoop, calls=%fused_computation.8 | loop fusion | flops 6291456 | bytes 50331648 | tf_op jit(solution)/shard_map/concatenate | solution.py:228
  652.6 12.9 broadcast_in_dim.126
  665.5 63.3 %scatter_fusion = f32[144,64,768]{2,1,0:T(8,128)} fusion(f32[144,64,768]{2,1,0:T(8,128)} %broadcast_in_dim.126, s32[128]{0:T(128)S(1)} %copy-done.63, f32[128,64,768]{2,1,0:T(8,128)} %pad_maximum_fusion), kind=kCustom, calls=%fused_computation.1 | custom fusion | flops 6291456 | bytes 75497984 | tf_op jit(solution)/shard_map/scatter-add | solution.py:237
  732.7 184.5 %while.43 = (s32[]{:T(128)}, f32[1024,768]{1,0:T(8,128)}, f32[1024,768]{1,0:T(8,128)}, f32[9,1024,768]{2,1,0:T(8,128)}, s32[]{:T(128)}, /*index=5*/s32[]{:T(128)}, s32[]{:T(128)}, s32[]{:T(128)}) while((s32[]{:T(128)}, f32[1024,768]{1,0:T(8,128)}, f32[1024,768]{1,0:T(8,128)}, f32[9,1024,768]{2,1,0:T(8,128)}, s32[]{:T(128)}, ...), condition=%wide.region_20.21_spmd.clone, body=%wide.region_19.20_spmd.clone.sunk | while | flops 6291463 | bytes 37748964 | solution.py:255
  738.9 32.9 %collective-permute-start.3 = (bf16[1024,768]{1,0:T(8,128)(2,1)S(1)}, bf16[1024,768]{1,0:T(8,128)(2,1)}, u32[]{:S(2)}, u32[]{:S(2)}) collective-permute-start(bf16[1024,768]{1,0:T(8,128)(2,1)S(1)} %get-tuple-element.426), channel_id=1, source_target_pairs={{0,2},{2,4},{4,6},{6,8},{8,10},{10,12},{12,14},{14,16},{16,18},{18... | collective-permute-start | bytes 4718600 | tf_op jit(solution)/shard_map/while/body/eval_jaxpr/ppermute | solution.py:15
  778.6 6.7 fusion.116
  786.6 35.1 %collective-permute-start.3 = (bf16[1024,768]{1,0:T(8,128)(2,1)S(1)}, bf16[1024,768]{1,0:T(8,128)(2,1)}, u32[]{:S(2)}, u32[]{:S(2)}) collective-permute-start(bf16[1024,768]{1,0:T(8,128)(2,1)S(1)} %get-tuple-element.426), channel_id=1, source_target_pairs={{0,2},{2,4},{4,6},{6,8},{8,10},{10,12},{12,14},{14,16},{16,18},{18... | collective-permute-start | bytes 4718600 | tf_op jit(solution)/shard_map/while/body/eval_jaxpr/ppermute | solution.py:15
  828.3 6.7 fusion.116
  836.3 35.9 %collective-permute-start.3 = (bf16[1024,768]{1,0:T(8,128)(2,1)S(1)}, bf16[1024,768]{1,0:T(8,128)(2,1)}, u32[]{:S(2)}, u32[]{:S(2)}) collective-permute-start(bf16[1024,768]{1,0:T(8,128)(2,1)S(1)} %get-tuple-element.426), channel_id=1, source_target_pairs={{0,2},{2,4},{4,6},{6,8},{8,10},{10,12},{12,14},{14,16},{16,18},{18... | collective-permute-start | bytes 4718600 | tf_op jit(solution)/shard_map/while/body/eval_jaxpr/ppermute | solution.py:15
  879.0 6.7 fusion.116
  886.9 23.6 %collective-permute-start.3 = (bf16[1024,768]{1,0:T(8,128)(2,1)S(1)}, bf16[1024,768]{1,0:T(8,128)(2,1)}, u32[]{:S(2)}, u32[]{:S(2)}) collective-permute-start(bf16[1024,768]{1,0:T(8,128)(2,1)S(1)} %get-tuple-element.426), channel_id=1, source_target_pairs={{0,2},{2,4},{4,6},{6,8},{8,10},{10,12},{12,14},{14,16},{16,18},{18... | collective-permute-start | bytes 4718600 | tf_op jit(solution)/shard_map/while/body/eval_jaxpr/ppermute | solution.py:15
  922.5 10.8 all_to_all.143
  938.5 11.5 all_to_all.144
  955.4 10.6 fusion.51
  967.5 7.2 fusion.70
  976.6 114.4 %all-reduce.5 = (bf16[768]{0:T(1024)(128)(2,1)S(1)}, bf16[768]{0:T(1024)(128)(2,1)S(1)}, bf16[768]{0:T(1024)(128)(2,1)S(1)}, bf16[768]{0:T(1024)(128)(2,1)S(1)}) all-reduce(f32[768]{0:T(1024)S(1)} %copy-done.49, f32[768]{0:T(1024)S(1)} %copy-done.50, f32[768]{0:T(1024)S(1)} %copy-done.29, ...), channel_id=6, replica_groups=mesh['seq'=16,'head'=2] {'seq'}, use_global_device_ids=true, to_apply=%region_30.31.clone | all-reduce | flops 3072 | bytes 18432
  1091.3 4.9 all-reduce.6
  1103.3 21.2 %reduce-scatter.23.cloned.1.call-done = f32[48,768]{1,0:T(8,128)} async-done(((f32[768,768]{1,0:T(8,128)}), f32[48,768]{1,0:T(8,128)}) %reduce-scatter.23.cloned.1.call-update) | async-done | bytes 147472
  1126.2 112.7 %reduce-scatter.17.cloned.1.call-done = f32[192,768]{1,0:T(8,128)} async-done(((f32[3072,768]{1,0:T(8,128)}), f32[192,768]{1,0:T(8,128)}) %reduce-scatter.17.cloned.1.call-update) | async-done | bytes 589840 | tf_op jit(solution)/shard_map/reduce_scatter | solution.py:292
  1240.7 113.9 %reduce-scatter.15.cloned.1.call-done = f32[48,3072]{1,0:T(8,128)} async-done(((f32[768,3072]{1,0:T(8,128)}), f32[48,3072]{1,0:T(8,128)}) %reduce-scatter.15.cloned.1.call-update) | async-done | bytes 589840 | tf_op jit(solution)/shard_map/reduce_scatter | solution.py:291
  1361.6 42.0 %all-reduce.10.cloned.1.call-done = (bf16[48,768]{0,1:T(8,128)(2,1)}, bf16[48,768]{0,1:T(8,128)(2,1)}, bf16[48,768]{0,1:T(8,128)(2,1)}, bf16[48,768]{1,0:T(8,128...) async-done(((bf16[48,768]{0,1:T(8,128)(2,1)}, bf16[48,768]{0,1:T(8,128)(2,1)}, bf16[48,768]{0,1:T(8,128)(2,1)}, bf16[48,768]{1,0:T(8,128)(2,1)}, ...) | async-done | bytes 884752 | tf_op jit(solution)/shard_map/psum | solution.py:297
  (332 shorter events, 226.6 us)
Async XLA Ops:
  7.2 361.3 %copy-start = (bf16[768,768]{1,0:T(8,128)(2,1)S(1)}, bf16[768,768]{1,0:T(8,128)(2,1)}, u32[]{:S(2)}) copy-start(bf16[768,768]{1,0:T(8,128)(2,1)} %param.23) | copy-start | bytes 3538948
  10.6 15.9 %all-to-all-start = ((bf16[512,2,384]{2,0,1:T(8,128)(2,1)}), bf16[512,2,384]{2,0,1:T(8,128)(2,1)S(1)}, u32[]{:S(2)}, u32[]{:S(2)}) async-start(bf16[512,2,384]{2,0,1:T(8,128)(2,1)} %bitcast.263), calls=%async_computation | async-start | bytes 1572864 | tf_op jit(solution)/shard_map/all_to_all | solution.py:148
  26.5 14.0 all-to-all-start.1
  40.6 244.5 %all-to-all-start.2 = ((bf16[512,2,384]{0,2,1:T(8,128)(2,1)}), bf16[512,2,384]{0,2,1:T(8,128)(2,1)}, u32[]{:S(2)}, u32[]{:S(2)}) async-start(bf16[512,2,384]{0,2,1:T(8,128)(2,1)} %bitcast.40), calls=%async_computation.2 | async-start | bytes 1572864 | tf_op jit(solution)/shard_map/all_to_all | solution.py:147
  54.8 4.5 collective-permute-start
  56.1 7.2 collective-permute-start.1
  70.0 35.6 %collective-permute-start = (bf16[1024,768]{1,0:T(8,128)(2,1)}, bf16[1024,768]{1,0:T(8,128)(2,1)S(1)}, u32[]{:S(2)}, u32[]{:S(2)}) collective-permute-start(bf16[1024,768]{1,0:T(8,128)(2,1)} %get-tuple-element.438), channel_id=1, source_target_pairs={{0,2},{2,4},{4,6},{6,8},{8,10},{10,12},{12,14},{14,16},{16,18},{18... | collective-permute-start | bytes 4718600 | tf_op jit(solution)/shard_map/while/body/eval_jaxpr/ppermute | solution.py:15
  102.5 7.4 collective-permute-start.1
  116.6 22.0 %collective-permute-start = (bf16[1024,768]{1,0:T(8,128)(2,1)}, bf16[1024,768]{1,0:T(8,128)(2,1)S(1)}, u32[]{:S(2)}, u32[]{:S(2)}) collective-permute-start(bf16[1024,768]{1,0:T(8,128)(2,1)} %get-tuple-element.438), channel_id=1, source_target_pairs={{0,2},{2,4},{4,6},{6,8},{8,10},{10,12},{12,14},{14,16},{16,18},{18... | collective-permute-start | bytes 4718600 | tf_op jit(solution)/shard_map/while/body/eval_jaxpr/ppermute | solution.py:15
  135.5 5.6 collective-permute-start.1
  147.8 36.2 %collective-permute-start = (bf16[1024,768]{1,0:T(8,128)(2,1)}, bf16[1024,768]{1,0:T(8,128)(2,1)S(1)}, u32[]{:S(2)}, u32[]{:S(2)}) collective-permute-start(bf16[1024,768]{1,0:T(8,128)(2,1)} %get-tuple-element.438), channel_id=1, source_target_pairs={{0,2},{2,4},{4,6},{6,8},{8,10},{10,12},{12,14},{14,16},{16,18},{18... | collective-permute-start | bytes 4718600 | tf_op jit(solution)/shard_map/while/body/eval_jaxpr/ppermute | solution.py:15
  180.9 5.6 collective-permute-start.1
  288.0 22.2 %copy-start.2 = (bf16[16,64,6,64]{1,0,3,2:T(8,128)(2,1)}, bf16[16,64,6,64]{1,0,3,2:T(8,128)(2,1)S(1)}, u32[]{:S(2)}) copy-start(bf16[16,64,6,64]{1,0,3,2:T(8,128)(2,1)S(1)} %reshape.690) | copy-start | bytes 2359300
  323.5 11.9 copy-start.21
  335.4 16.8 %copy-start.23 = (f32[16,6,64]{2,1,0:T(8,128)}, f32[16,6,64]{2,1,0:T(8,128)S(1)}, u32[]{:S(2)}) copy-start(f32[16,6,64]{2,1,0:T(8,128)S(1)} %fusion.2) | copy-start | bytes 73732
  353.3 15.2 %copy-start.7 = (bf16[512,768]{1,0:T(8,128)(2,1)S(1)}, bf16[512,768]{1,0:T(8,128)(2,1)}, u32[]{:S(2)}) copy-start(bf16[512,768]{1,0:T(8,128)(2,1)} %param.19) | copy-start | bytes 2359300
  356.9 11.5 all-to-all-start.3
  369.4 24.4 %copy-start.11 = (f32[512,768]{1,0:T(8,128)}, f32[512,768]{1,0:T(8,128)S(1)}, u32[]{:S(2)}) copy-start(f32[512,768]{1,0:T(8,128)S(1)} %get-tuple-element.363) | copy-start | bytes 4718596
  369.4 24.4 %copy-start.25 = (f32[512]{0:T(512)}, f32[512]{0:T(512)S(1)}, u32[]{:S(2)}) copy-start(f32[512]{0:T(512)S(1)} %broadcast_multiply_fusion.5) | copy-start | bytes 6148
  369.7 24.1 %copy-start.35 = (f32[512]{0:T(512)}, f32[512]{0:T(512)S(1)}, u32[]{:S(2)}) copy-start(f32[512]{0:T(512)S(1)} %add_rsqrt_fusion.1) | copy-start | bytes 6148
  375.2 14.7 %slice-start.2 = ((s8[4718592]{0:T(1024)(128)(4,1)}), s8[4194304]{0:T(1024)(128)(4,1)S(1)}, s32[]{:S(2)}) async-start(s8[4718592]{0:T(1024)(128)(4,1)} %bitcast.309), calls=%async_computation.23 | async-start | bytes 8388608
  379.1 10.7 copy-start.10
  379.2 10.7 copy-start.27
  394.3 19.2 %copy-start.4 = (f32[512,768]{1,0:T(8,128)}, f32[512,768]{1,0:T(8,128)S(1)}, u32[]{:S(2)}) copy-start(f32[512,768]{1,0:T(8,128)S(1)} %subtract_multiply_fusion) | copy-start | bytes 4718596
  398.3 17.4 %all-to-all-start.4 = ((bf16[512,2,384]{0,2,1:T(8,128)(2,1)}), bf16[512,2,384]{0,2,1:T(8,128)(2,1)S(1)}, u32[]{:S(2)}, u32[]{:S(2)}) async-start(bf16[512,2,384]{0,2,1:T(8,128)(2,1)} %bitcast.285), calls=%async_computation.4 | async-start | bytes 1572864 | tf_op jit(solution)/shard_map/all_to_all | solution.py:204
  401.9 696.4 %reduce-scatter.13.cloned.1.call-start = ((), (), s32[]{:S(2)}) async-start(), calls=%async_computation.14 | async-start | bytes 2506752 | tf_op jit(solution)/shard_map/reduce_scatter | solution.py:288
  480.3 149.9 %all-to-all-start.5 = ((bf16[2,512,384]{1,2,0:T(8,128)(2,1)}), bf16[2,512,384]{1,2,0:T(8,128)(2,1)S(1)}, u32[]{:S(2)}, u32[]{:S(2)}) async-start(bf16[2,512,384]{1,2,0:T(8,128)(2,1)} %copy.185), calls=%async_computation.5 | async-start | bytes 1572864 | tf_op jit(solution)/shard_map/all_to_all | solution.py:262
  483.9 615.9 %reduce-scatter.19.cloned.1.call-start = ((), (), s32[]{:S(2)}) async-start(), calls=%async_computation.17 | async-start | bytes 2506752
  483.9 25.2 %copy-start.3 = (bf16[16,64,6,64]{1,0,3,2:T(8,128)(2,1)S(1)}, bf16[16,64,6,64]{1,0,3,2:T(8,128)(2,1)}, u32[]{:S(2)}) copy-start(bf16[16,64,6,64]{1,0,3,2:T(8,128)(2,1)} %copy-done.2) | copy-start | bytes 2359300
  605.1 26.1 %copy-start.8 = (bf16[512,768]{1,0:T(8,128)(2,1)S(1)}, bf16[512,768]{1,0:T(8,128)(2,1)}, u32[]{:S(2)}) copy-start(bf16[512,768]{1,0:T(8,128)(2,1)} %param.19) | copy-start | bytes 2359300
  635.1 466.5 %reduce-scatter.21.cloned.1.call-start = ((), (), s32[]{:S(2)}) async-start(), calls=%async_computation.18 | async-start | bytes 2506752
  652.6 12.9 copy-start.63
  737.7 34.3 %collective-permute-start.2 = (bf16[1024,768]{1,0:T(8,128)(2,1)}, bf16[1024,768]{1,0:T(8,128)(2,1)}, u32[]{:S(2)}, u32[]{:S(2)}) collective-permute-start(bf16[1024,768]{1,0:T(8,128)(2,1)} %get-tuple-element.425), channel_id=1, source_target_pairs={{2,0},{4,2},{6,4},{8,6},{10,8},{12,10},{14,12},{16,14},{18,16},{20... | collective-permute-start | bytes 4718600 | tf_op jit(solution)/shard_map/while/body/eval_jaxpr/ppermute | solution.py:15
  738.9 36.3 %collective-permute-start.3 = (bf16[1024,768]{1,0:T(8,128)(2,1)S(1)}, bf16[1024,768]{1,0:T(8,128)(2,1)}, u32[]{:S(2)}, u32[]{:S(2)}) collective-permute-start(bf16[1024,768]{1,0:T(8,128)(2,1)S(1)} %get-tuple-element.426), channel_id=1, source_target_pairs={{0,2},{2,4},{4,6},{6,8},{8,10},{10,12},{12,14},{14,16},{16,18},{18... | collective-permute-start | bytes 4718600 | tf_op jit(solution)/shard_map/while/body/eval_jaxpr/ppermute | solution.py:15
  785.3 36.5 %collective-permute-start.2 = (bf16[1024,768]{1,0:T(8,128)(2,1)}, bf16[1024,768]{1,0:T(8,128)(2,1)}, u32[]{:S(2)}, u32[]{:S(2)}) collective-permute-start(bf16[1024,768]{1,0:T(8,128)(2,1)} %get-tuple-element.425), channel_id=1, source_target_pairs={{2,0},{4,2},{6,4},{8,6},{10,8},{12,10},{14,12},{16,14},{18,16},{20... | collective-permute-start | bytes 4718600 | tf_op jit(solution)/shard_map/while/body/eval_jaxpr/ppermute | solution.py:15
  786.6 38.5 %collective-permute-start.3 = (bf16[1024,768]{1,0:T(8,128)(2,1)S(1)}, bf16[1024,768]{1,0:T(8,128)(2,1)}, u32[]{:S(2)}, u32[]{:S(2)}) collective-permute-start(bf16[1024,768]{1,0:T(8,128)(2,1)S(1)} %get-tuple-element.426), channel_id=1, source_target_pairs={{0,2},{2,4},{4,6},{6,8},{8,10},{10,12},{12,14},{14,16},{16,18},{18... | collective-permute-start | bytes 4718600 | tf_op jit(solution)/shard_map/while/body/eval_jaxpr/ppermute | solution.py:15
  835.0 37.3 %collective-permute-start.2 = (bf16[1024,768]{1,0:T(8,128)(2,1)}, bf16[1024,768]{1,0:T(8,128)(2,1)}, u32[]{:S(2)}, u32[]{:S(2)}) collective-permute-start(bf16[1024,768]{1,0:T(8,128)(2,1)} %get-tuple-element.425), channel_id=1, source_target_pairs={{2,0},{4,2},{6,4},{8,6},{10,8},{12,10},{14,12},{16,14},{18,16},{20... | collective-permute-start | bytes 4718600 | tf_op jit(solution)/shard_map/while/body/eval_jaxpr/ppermute | solution.py:15
  836.3 39.3 %collective-permute-start.3 = (bf16[1024,768]{1,0:T(8,128)(2,1)S(1)}, bf16[1024,768]{1,0:T(8,128)(2,1)}, u32[]{:S(2)}, u32[]{:S(2)}) collective-permute-start(bf16[1024,768]{1,0:T(8,128)(2,1)S(1)} %get-tuple-element.426), channel_id=1, source_target_pairs={{0,2},{2,4},{4,6},{6,8},{8,10},{10,12},{12,14},{14,16},{16,18},{18... | collective-permute-start | bytes 4718600 | tf_op jit(solution)/shard_map/while/body/eval_jaxpr/ppermute | solution.py:15
  885.6 25.0 %collective-permute-start.2 = (bf16[1024,768]{1,0:T(8,128)(2,1)}, bf16[1024,768]{1,0:T(8,128)(2,1)}, u32[]{:S(2)}, u32[]{:S(2)}) collective-permute-start(bf16[1024,768]{1,0:T(8,128)(2,1)} %get-tuple-element.425), channel_id=1, source_target_pairs={{2,0},{4,2},{6,4},{8,6},{10,8},{12,10},{14,12},{16,14},{18,16},{20... | collective-permute-start | bytes 4718600 | tf_op jit(solution)/shard_map/while/body/eval_jaxpr/ppermute | solution.py:15
  886.9 27.0 %collective-permute-start.3 = (bf16[1024,768]{1,0:T(8,128)(2,1)S(1)}, bf16[1024,768]{1,0:T(8,128)(2,1)}, u32[]{:S(2)}, u32[]{:S(2)}) collective-permute-start(bf16[1024,768]{1,0:T(8,128)(2,1)S(1)} %get-tuple-element.426), channel_id=1, source_target_pairs={{0,2},{2,4},{4,6},{6,8},{8,10},{10,12},{12,14},{14,16},{16,18},{18... | collective-permute-start | bytes 4718600 | tf_op jit(solution)/shard_map/while/body/eval_jaxpr/ppermute | solution.py:15
  938.4 186.1 %reduce-scatter.23.cloned.1.call-start = ((), (), s32[]{:S(2)}) async-start(), calls=%async_computation.19 | async-start | bytes 2506752
  955.1 283.8 %reduce-scatter.17.cloned.1.call-start = ((), (), s32[]{:S(2)}) async-start(), calls=%async_computation.16 | async-start | bytes 10027008 | tf_op jit(solution)/shard_map/reduce_scatter | solution.py:292
  966.1 388.4 %reduce-scatter.15.cloned.1.call-start = ((), (), s32[]{:S(2)}) async-start(), calls=%async_computation.15 | async-start | bytes 10027008 | tf_op jit(solution)/shard_map/reduce_scatter | solution.py:291
  974.7 381.7 %copy-start.16 = (bf16[2,512,384]{1,2,0:T(8,128)(2,1)S(1)}, bf16[2,512,384]{1,2,0:T(8,128)(2,1)}, u32[]{:S(2)}) copy-start(bf16[2,512,384]{1,2,0:T(8,128)(2,1)} %copy-done.15) | copy-start | bytes 2359300
  974.7 381.7 %copy-start.64 = (bf16[768,768]{1,0:T(8,128)(2,1)S(1)}, bf16[768,768]{1,0:T(8,128)(2,1)}, u32[]{:S(2)}) copy-start(bf16[768,768]{1,0:T(8,128)(2,1)} %param.20) | copy-start | bytes 3538948
  974.7 428.9 %all-reduce.10.cloned.1.call-start = ((), (), s32[]{:S(2)}) async-start(), calls=%async_computation.20 | async-start | bytes 2506752 | tf_op jit(solution)/shard_map/psum | solution.py:297
  1240.7 116.6 %copy-start.17 = (bf16[512,2,384]{0,2,1:T(8,128)(2,1)S(1)}, bf16[512,2,384]{0,2,1:T(8,128)(2,1)}, u32[]{:S(2)}) copy-start(bf16[512,2,384]{0,2,1:T(8,128)(2,1)} %copy.194) | copy-start | bytes 2359300
  1359.6 54.3 %copy-start.1 = (bf16[768,768]{1,0:T(8,128)(2,1)S(1)}, bf16[768,768]{1,0:T(8,128)(2,1)}, u32[]{:S(2)}) copy-start(bf16[768,768]{1,0:T(8,128)(2,1)} %param.23) | copy-start | bytes 3538948
  (57 other events, 232.7 us)
Sparse Core Ops, SparseCore 0:
  415.9 115.2 reduce-scatter.12
  635.2 115.9 reduce-scatter.18
  938.5 119.8 reduce-scatter.20
  1062.6 61.9 reduce-scatter.22
  1128.5 110.3 reduce-scatter.16
  1243.4 111.1 reduce-scatter.14
  1358.3 45.1 all-reduce.9
where the time goes:
time: 1430 us; the launch traced here: 1420 us
  local copies, waits for them, and re-layouts  338 us (24%)
  waiting for transfers between devices  322 us (23%)
  starting transfers between devices  247 us (17%)
  other arithmetic  192 us (13%)
  matrix products  164 us (11%)
  blocking collectives  142 us (10%)
  between operations  16.2 us (1%)
    ppermute x16, starting transfers between devices, shifted(): lax.ppermute(value, axis, [(source, source + steps) for source in range(f...  224 us
    unnamed x1, blocking collectives  114 us
    reduce_scatter x1, waiting for transfers between devices, body(): lax.psum_scatter(grad_terms[6], 'seq', scatter_dimension=0, tiled=True)  114 us
    reduce_scatter x1, waiting for transfers between devices, body(): lax.psum_scatter(grad_terms[7], 'seq', scatter_dimension=0, tiled=True)  113 us
    scatter-add x1, other arithmetic, body(): grad_buffer.at[local_rows.reshape(-1)]  63.3 us
    unnamed x169, local copies, waits for them, and re-layouts  56 us
    concatenate x2, local copies, waits for them, and re-layouts, body(): jnp.concatenate([grad_key_rows.reshape(stretch_blocks, slot_count, BLK, -...  50.3 us
    psum x1, waiting for transfers between devices, body(): lax.psum(shares[0].astype(jnp.bfloat16), 'head').astype(jnp.float32)  42 us
  transfers between devices with their start and end apart: 29, of which 19 were waited for; matrix products, arithmetic and copies ran while one was open for 40% of the time, Pallas kernels for 0%

commit v1 on v0

--- a/solution.py
+++ b/solution.py
@@ -294,7 +294,7 @@
         lax.psum_scatter(grad_terms[9], "seq", scatter_dimension=0, tiled=True),
     )
     totals = (
-        lax.psum(shares[0].astype(jnp.bfloat16), "head").astype(jnp.float32),
+        jnp.sum(lax.all_gather(shares[0].astype(jnp.bfloat16), "head"), axis=0).astype(jnp.float32),
         lax.psum(shares[1].astype(jnp.bfloat16), "head").astype(jnp.float32),
         lax.psum(shares[2].astype(jnp.bfloat16), "head").astype(jnp.float32),
         lax.psum(shares[3].astype(jnp.bfloat16), "head").astype(jnp.float32),

time: 1430 us -> 1480 us (1.035)
  waiting for transfers between devices: 322 us -> 352 us
  starting transfers between devices: 247 us -> 267 us
    reduce_scatter x0 -> x1, waiting for transfers between devices: none -> 59.8 us  [body(): lax.psum_scatter(grad_terms[0], 'seq', scatter_dimension=0, tiled=True)]
    ppermute x16, starting transfers between devices: 224 us -> 248 us  [shifted(): lax.ppermute(value, axis, [(source, source + steps) for source in range(f...]
    unnamed x10 -> x9, waiting for transfers between devices: 21.3 us -> 2.77 us
    unnamed x169 -> x165, local copies, waits for them, and re-layouts: 56 us -> 52.9 us
  transfers between devices with their start and end apart: 29 -> 28, of which waited for: 19 -> 16; matrix products, arithmetic and copies ran while one was open for 40% -> 30% of each run, Pallas kernels for 0% -> 0%
where the time goes in v1:
time: 1480 us; the launch traced here: 1470 us
  waiting for transfers between devices  352 us (24%)
  local copies, waits for them, and re-layouts  336 us (23%)
  starting transfers between devices  267 us (18%)
  other arithmetic  193 us (13%)
  matrix products  162 us (11%)
  blocking collectives  147 us (10%)
  between operations  16.1 us (1%)
    ppermute x16, starting transfers between devices, shifted(): lax.ppermute(value, axis, [(source, source + steps) for source in range(f...  248 us
    reduce_scatter x1, waiting for transfers between devices, body(): lax.psum_scatter(grad_terms[6], 'seq', scatter_dimension=0, tiled=True)  113 us
    reduce_scatter x1, waiting for transfers between devices, body(): lax.psum_scatter(grad_terms[7], 'seq', scatter_dimension=0, tiled=True)  113 us
    unnamed x1, blocking collectives  100 us
    scatter-add x1, other arithmetic, body(): grad_buffer.at[local_rows.reshape(-1)]  63.2 us
    reduce_scatter x1, waiting for transfers between devices, body(): lax.psum_scatter(grad_terms[0], 'seq', scatter_dimension=0, tiled=True)  59.8 us
    unnamed x165, local copies, waits for them, and re-layouts  52.9 us
    concatenate x2, local copies, waits for them, and re-layouts, body(): jnp.concatenate([grad_key_rows.reshape(stretch_blocks, slot_count, BLK, -...  50.4 us
  transfers between devices with their start and end apart: 28, of which 16 were waited for; matrix products, arithmetic and copies ran while one was open for 30% of the time, Pallas kernels for 0%

profile of v1, /device:TPU:0, one launch (start us, length us, event | category | flops | bytes accessed | tf_op | source)
XLA Modules:
  0.0 1473.0 jit_solution(799116442904613278)
XLA Ops:
  20.6 6.0 all-to-all-done.2
  33.1 7.7 all-to-all-done
  61.1 6.0 dynamic_update_slice.22
  67.1 151.4 %while.42 = (s32[]{:T(128)}, bf16[1024,768]{1,0:T(8,128)(2,1)}, bf16[1024,768]{1,0:T(8,128)(2,1)}, bf16[9,1024,768]{2,1,0:T(8,128)(2,1)}, s32[]{:T(128)}, /*inde...) while((s32[]{:T(128)}, bf16[1024,768]{1,0:T(8,128)(2,1)}, bf16[1024,768]{1,0:T(8,128)(2,1)}, ...), condition=%wide.region_1.2_spmd, body=%wide.region_0.1_spmd.sunk | while | flops 10 | bytes 25166108 | solution.py:105
  82.7 50.9 %collective-permute-start = (bf16[1024,768]{1,0:T(8,128)(2,1)}, bf16[1024,768]{1,0:T(8,128)(2,1)}, u32[]{:S(2)}, u32[]{:S(2)}) collective-permute-start(bf16[1024,768]{1,0:T(8,128)(2,1)} %get-tuple-element.449), channel_id=1, source_target_pairs={{0,2},{2,4},{4,6},{6,8},{8,10},{10,12},{12,14},{14,16},{16,18},{18... | collective-permute-start | bytes 4718600 | tf_op jit(solution)/shard_map/while/body/eval_jaxpr/ppermute | solution.py:15
  143.6 20.5 %collective-permute-start = (bf16[1024,768]{1,0:T(8,128)(2,1)}, bf16[1024,768]{1,0:T(8,128)(2,1)}, u32[]{:S(2)}, u32[]{:S(2)}) collective-permute-start(bf16[1024,768]{1,0:T(8,128)(2,1)} %get-tuple-element.449), channel_id=1, source_target_pairs={{0,2},{2,4},{4,6},{6,8},{8,10},{10,12},{12,14},{14,16},{16,18},{18... | collective-permute-start | bytes 4718600 | tf_op jit(solution)/shard_map/while/body/eval_jaxpr/ppermute | solution.py:15
  174.3 35.4 %collective-permute-start = (bf16[1024,768]{1,0:T(8,128)(2,1)}, bf16[1024,768]{1,0:T(8,128)(2,1)}, u32[]{:S(2)}, u32[]{:S(2)}) collective-permute-start(bf16[1024,768]{1,0:T(8,128)(2,1)} %get-tuple-element.449), channel_id=1, source_target_pairs={{0,2},{2,4},{4,6},{6,8},{8,10},{10,12},{12,14},{14,16},{16,18},{18... | collective-permute-start | bytes 4718600 | tf_op jit(solution)/shard_map/while/body/eval_jaxpr/ppermute | solution.py:15
  218.4 13.2 gather_fusion
  231.7 39.0 %reshape.689 = bf16[16,8,64,2,6,64]{5,4,3,2,1,0:T(8,128)(2,1)} reshape(bf16[128,64,768]{2,1,0:T(8,128)(2,1)} %gather_fusion) | data formatting | bytes 25165824 | tf_op jit(solution)/shard_map/reshape | solution.py:112
  270.7 28.5 %slice_bitcast_fusion = (bf16[16,8,64,6,64]{4,3,2,1,0:T(8,128)(2,1)}, bf16[16,8,64,1,6,64]{5,4,3,2,1,0:T(8,128)(2,1)}, bf16[16,8,64,1,6,64]{5,4,3,2,1,0:T(8,128)(2,1)}) fusion(bf16[16,8,64,2,6,64]{5,4,3,2,1,0:T(8,128)(2,1)} %reshape.689), kind=kLoop, calls=%fused_computation.149 | loop fusion | bytes 31457280 | tf_op jit(solution)/shard_map/squeeze | solution.py:113
  299.1 11.3 copy.267
  310.4 21.7 %copy.266 = bf16[16,8,64,1,6,64]{2,5,1,4,0,3:T(8,128)(2,1)} copy(bf16[16,8,64,1,6,64]{5,4,3,2,1,0:T(8,128)(2,1)} %get-tuple-element.354) | data formatting | bytes 12582912
  332.1 13.3 fusion.11
  345.4 11.9 fusion.2
  357.3 16.6 %fusion.44 = bf16[16,64,6,64]{1,3,2,0:T(8,128)(2,1)S(1)} fusion(f32[16,6,64]{2,1,0:T(8,128)S(1)} %fusion.2, f32[16,6,64]{2,1,0:T(8,128)S(1)} %get-tuple-element.371, f32[16,6,64,8,64]{2,4,3,1,0:T(8,128)} %bitcast.271, pred[16,8]{1,0:T(8,128)(4,1)S(1)} %copy.215, bf16[16,8,64,1,6,64]{2,5,1,4,0,3:T(8,128)(2,1)} %copy.266), kind=kOutput, calls=%fused_computation.71 | convolution fusion | flops 418775040 | bytes 19710080 | tf_op jit(solution)/shard_map/chqsk,cskhd->cqhd/dot_general | solution.py:172
  383.0 7.2 all-to-all-done.3
  403.5 8.1 fusion.21
  423.7 11.6 copy.226
  439.4 24.1 %multiply_reduce_fusion = (f32[16,6,64]{2,1,0:T(8,128)S(1)}, f32[16,6,64,512]{2,3,1,0}) fusion(f32[16,6,64]{2,1,0:T(8,128)S(1)} %log_add_fusion, pred[16,8]{1,0:T(8,128)(4,1)S(1)} %copy.215, f32[16,6,64,512]{2,3,1,0} %get-tuple-element.372, bf16[16,6,64,512]{2,3,1,0:T(8,128)(2,1)} %bitcast.276, bf16[16,64,6,64]{1,0,3,2:T(8,128)(2,1)S(1)} %reshape.691), kind=kOutput, calls=%fused_computation.11 | convolution fusion | flops 418375680 | bytes 32292992
  463.6 24.4 %fusion.12 = f32[16,8,64,6,64]{2,4,1,3,0:T(8,128)} fusion(f32[16,6,64]{2,1,0:T(8,128)S(1)} %log_add_fusion, f32[16,6,64,8,64]{2,4,3,1,0:T(8,128)} %bitcast.272, pred[16,8]{1,0:T(8,128)(4,1)S(1)} %copy.215, bf16[16,64,6,64,1]{1,0,3,2,4:T(8,128)(2,1)S(1)} %bitcast.278), kind=kOutput, calls=%fused_computation.27 | convolution fusion | flops 415236096 | bytes 25976960 | tf_op jit(solution)/shard_map/chqsk,cqhd->cskhd/dot_general | solution.py:215
  488.0 29.1 %copy.238 = f32[16,8,64,6,64]{4,3,2,1,0:T(8,128)} copy(f32[16,8,64,6,64]{2,4,1,3,0:T(8,128)} %fusion.12) | data formatting | bytes 25165824 | tf_op jit(solution)/shard_map/chqsk,cqhd->cskhd/transpose | solution.py:215
  517.0 25.2 %concatenate.52 = f32[128,64,384]{2,1,0:T(8,128)} reshape(f32[16,8,64,6,64]{4,3,2,1,0:T(8,128)} %copy.238) | data formatting | bytes 25165824 | tf_op jit(solution)/shard_map/concatenate | solution.py:228
  542.3 22.0 %multiply_convert_fusion = bf16[16,6,64,8,64]{2,4,3,1,0:T(8,128)(2,1)} fusion(f32[16,6,64]{2,1,0:T(8,128)S(1)} %get-tuple-element.378, f32[16,6,64]{2,1,0:T(8,128)S(1)} %log_add_fusion, pred[16,8]{1,0:T(8,128)(4,1)S(1)} %copy.215, f32[16,6,64,512]{2,3,1,0} %get-tuple-element.379, f32[16,6,64,512]{2,3,1,0} %get-tuple-element.372), kind=kLoop, calls=%fused_computation.10 | loop fusion | flops 18874368 | bytes 31506560 | tf_op jit(solution)/shard_map/convert_element_type | solution.py:219
  564.2 12.9 multiply_bitcast_fusion
  577.1 29.5 %copy.235 = f32[16,8,64,6,64]{4,3,2,1,0:T(8,128)} copy(f32[16,8,64,6,64]{4,2,1,3,0:T(8,128)} %multiply_bitcast_fusion) | data formatting | bytes 25165824 | tf_op jit(solution)/shard_map/mul | solution.py:225
  606.6 25.1 %concatenate.51 = f32[128,64,384]{2,1,0:T(8,128)} reshape(f32[16,8,64,6,64]{4,3,2,1,0:T(8,128)} %copy.235) | data formatting | bytes 25165824 | tf_op jit(solution)/shard_map/concatenate | solution.py:228
  631.8 17.4 %pad_maximum_fusion = f32[128,64,768]{2,1,0:T(8,128)} fusion(f32[128,64,384]{2,1,0:T(8,128)} %concatenate.52, f32[128,64,384]{2,1,0:T(8,128)} %concatenate.51), kind=kLoop, calls=%fused_computation.8 | loop fusion | flops 6291456 | bytes 50331648 | tf_op jit(solution)/shard_map/concatenate | solution.py:228
  649.1 12.9 broadcast_in_dim.126
  662.0 63.2 %scatter_fusion = f32[144,64,768]{2,1,0:T(8,128)} fusion(f32[144,64,768]{2,1,0:T(8,128)} %broadcast_in_dim.126, s32[128]{0:T(128)S(1)} %copy-done.62, f32[128,64,768]{2,1,0:T(8,128)} %pad_maximum_fusion), kind=kCustom, calls=%fused_computation.1 | custom fusion | flops 6291456 | bytes 75497984 | tf_op jit(solution)/shard_map/scatter-add | solution.py:237
  729.0 184.3 %while.43 = (s32[]{:T(128)}, f32[1024,768]{1,0:T(8,128)}, f32[1024,768]{1,0:T(8,128)}, f32[9,1024,768]{2,1,0:T(8,128)}, s32[]{:T(128)}, /*index=5*/s32[]{:T(128)}, s32[]{:T(128)}, s32[]{:T(128)}) while((s32[]{:T(128)}, f32[1024,768]{1,0:T(8,128)}, f32[1024,768]{1,0:T(8,128)}, f32[9,1024,768]{2,1,0:T(8,128)}, s32[]{:T(128)}, ...), condition=%wide.region_20.21_spmd.clone, body=%wide.region_19.20_spmd.clone.sunk | while | flops 6291463 | bytes 37748964 | solution.py:255
  735.2 35.0 %collective-permute-start.3 = (bf16[1024,768]{1,0:T(8,128)(2,1)S(1)}, bf16[1024,768]{1,0:T(8,128)(2,1)}, u32[]{:S(2)}, u32[]{:S(2)}) collective-permute-start(bf16[1024,768]{1,0:T(8,128)(2,1)S(1)} %get-tuple-element.437), channel_id=1, source_target_pairs={{0,2},{2,4},{4,6},{6,8},{8,10},{10,12},{12,14},{14,16},{16,18},{18... | collective-permute-start | bytes 4718600 | tf_op jit(solution)/shard_map/while/body/eval_jaxpr/ppermute | solution.py:15
  776.9 6.7 fusion.116
  784.9 36.3 %collective-permute-start.3 = (bf16[1024,768]{1,0:T(8,128)(2,1)S(1)}, bf16[1024,768]{1,0:T(8,128)(2,1)}, u32[]{:S(2)}, u32[]{:S(2)}) collective-permute-start(bf16[1024,768]{1,0:T(8,128)(2,1)S(1)} %get-tuple-element.437), channel_id=1, source_target_pairs={{0,2},{2,4},{4,6},{6,8},{8,10},{10,12},{12,14},{14,16},{16,18},{18... | collective-permute-start | bytes 4718600 | tf_op jit(solution)/shard_map/while/body/eval_jaxpr/ppermute | solution.py:15
  828.0 6.7 fusion.116
  836.0 21.6 %collective-permute-start.3 = (bf16[1024,768]{1,0:T(8,128)(2,1)S(1)}, bf16[1024,768]{1,0:T(8,128)(2,1)}, u32[]{:S(2)}, u32[]{:S(2)}) collective-permute-start(bf16[1024,768]{1,0:T(8,128)(2,1)S(1)} %get-tuple-element.437), channel_id=1, source_target_pairs={{0,2},{2,4},{4,6},{6,8},{8,10},{10,12},{12,14},{14,16},{16,18},{18... | collective-permute-start | bytes 4718600 | tf_op jit(solution)/shard_map/while/body/eval_jaxpr/ppermute | solution.py:15
  864.4 6.7 fusion.116
  872.4 34.1 %collective-permute-start.3 = (bf16[1024,768]{1,0:T(8,128)(2,1)S(1)}, bf16[1024,768]{1,0:T(8,128)(2,1)}, u32[]{:S(2)}, u32[]{:S(2)}) collective-permute-start(bf16[1024,768]{1,0:T(8,128)(2,1)S(1)} %get-tuple-element.437), channel_id=1, source_target_pairs={{0,2},{2,4},{4,6},{6,8},{8,10},{10,12},{12,14},{14,16},{16,18},{18... | collective-permute-start | bytes 4718600 | tf_op jit(solution)/shard_map/while/body/eval_jaxpr/ppermute | solution.py:15
  918.6 11.2 all_to_all.143
  934.9 15.1 %all_to_all.144 = bf16[2,512,384]{2,1,0:T(8,128)(2,1)S(1)} all-to-all(bf16[2,512,384]{2,1,0:T(8,128)(2,1)} %bitcast.292), channel_id=1, replica_groups=mesh['seq'=16,'head'=2] {'head'}, dimensions={0} | all-to-all | bytes 1572864 | tf_op jit(solution)/shard_map/all_to_all | solution.py:263
  955.3 10.8 fusion.51
  967.6 7.2 fusion.70
  974.9 10.7 fusion.41
  987.5 10.4 all_to_all.145
  1003.0 100.4 %all-reduce.5 = (bf16[768]{0:T(1024)(128)(2,1)S(1)}, bf16[768]{0:T(1024)(128)(2,1)S(1)}, bf16[768]{0:T(1024)(128)(2,1)S(1)}, bf16[768]{0:T(1024)(128)(2,1)S(1)}) all-reduce(f32[768]{0:T(1024)S(1)} %copy-done.49, f32[768]{0:T(1024)S(1)} %copy-done.50, f32[768]{0:T(1024)S(1)} %copy-done.29, ...), channel_id=7, replica_groups=mesh['seq'=16,'head'=2] {'seq'}, use_global_device_ids=true, to_apply=%region_30.31.clone | all-reduce | flops 3072 | bytes 18432
  1118.5 113.2 %reduce-scatter.17.cloned.1.call-done = f32[192,768]{1,0:T(8,128)} async-done(((f32[3072,768]{1,0:T(8,128)}), f32[192,768]{1,0:T(8,128)}) %reduce-scatter.17.cloned.1.call-update) | async-done | bytes 589840 | tf_op jit(solution)/shard_map/reduce_scatter | solution.py:292
  1233.5 113.3 %reduce-scatter.15.cloned.1.call-done = f32[48,3072]{1,0:T(8,128)} async-done(((f32[768,3072]{1,0:T(8,128)}), f32[48,3072]{1,0:T(8,128)}) %reduce-scatter.15.cloned.1.call-update) | async-done | bytes 589840 | tf_op jit(solution)/shard_map/reduce_scatter | solution.py:291
  1353.8 59.8 %reduce-scatter.19.cloned.1.call-done = f32[48,768]{1,0:T(8,128)} async-done(((f32[768,768]{1,0:T(8,128)}), f32[48,768]{1,0:T(8,128)}) %reduce-scatter.19.cloned.1.call-update) | async-done | bytes 147472 | tf_op jit(solution)/shard_map/reduce_scatter | solution.py:285
  1420.3 37.1 %all-reduce.10.cloned.1.call-done = (bf16[48,768]{0,1:T(8,128)(2,1)}, bf16[48,768]{0,1:T(8,128)(2,1)}, bf16[48,768]{1,0:T(8,128)(2,1)}, bf16[48,3072]{1,0:T(8,128)(2,1)}, bf16[192,768]{1,0:T(8,128)(2,1)}) async-done(((bf16[48,768]{0,1:T(8,128)(2,1)}, bf16[48,768]{0,1:T(8,128)(2,1)}, bf16[48,768]{1,0:T(8,128)(2,1)}, bf16[48,3072]{1,0:T(8,128)(2,1)}, bf16[192,768]{1,0:T(8,128)(2,1)}), ...) | async-done | bytes 811024 | tf_op jit(solution)/shard_map/psum | solution.py:298
  (331 shorter events, 225.9 us)
Async XLA Ops:
  7.2 383.0 %copy-start = (bf16[768,768]{1,0:T(8,128)(2,1)S(1)}, bf16[768,768]{1,0:T(8,128)(2,1)}, u32[]{:S(2)}) copy-start(bf16[768,768]{1,0:T(8,128)(2,1)} %param.23) | copy-start | bytes 3538948
  10.8 15.8 %all-to-all-start.2 = ((bf16[512,2,384]{0,2,1:T(8,128)(2,1)}), bf16[512,2,384]{0,2,1:T(8,128)(2,1)S(1)}, u32[]{:S(2)}, u32[]{:S(2)}) async-start(bf16[512,2,384]{0,2,1:T(8,128)(2,1)} %bitcast.40), calls=%async_computation.2 | async-start | bytes 1572864 | tf_op jit(solution)/shard_map/all_to_all | solution.py:147
  15.6 17.4 %copy-start.32 = (s32[16]{0:T(128)}, s32[16]{0:T(128)S(1)}, u32[]{:S(2)}) copy-start(s32[16]{0:T(128)S(1)} %get-tuple-element.311) | copy-start | bytes 196
  26.6 14.2 all-to-all-start
  33.0 13.5 copy-start.39
  40.8 15.8 %all-to-all-start.1 = ((bf16[512,2,384]{2,0,1:T(8,128)(2,1)}), bf16[512,2,384]{2,0,1:T(8,128)(2,1)S(1)}, u32[]{:S(2)}, u32[]{:S(2)}) async-start(bf16[512,2,384]{2,0,1:T(8,128)(2,1)} %bitcast.286), calls=%async_computation.1 | async-start | bytes 1572864 | tf_op jit(solution)/shard_map/all_to_all | solution.py:149
  67.1 5.5 collective-permute-start.1
  68.3 6.4 collective-permute-start
  81.4 52.2 %collective-permute-start.1 = (bf16[1024,768]{1,0:T(8,128)(2,1)}, bf16[1024,768]{1,0:T(8,128)(2,1)S(1)}, u32[]{:S(2)}, u32[]{:S(2)}) collective-permute-start(bf16[1024,768]{1,0:T(8,128)(2,1)} %get-tuple-element.450), channel_id=1, source_target_pairs={{2,0},{4,2},{6,4},{8,6},{10,8},{12,10},{14,12},{16,14},{18,16},{20... | collective-permute-start | bytes 4718600 | tf_op jit(solution)/shard_map/while/body/eval_jaxpr/ppermute | solution.py:15
  82.7 53.1 %collective-permute-start = (bf16[1024,768]{1,0:T(8,128)(2,1)}, bf16[1024,768]{1,0:T(8,128)(2,1)}, u32[]{:S(2)}, u32[]{:S(2)}) collective-permute-start(bf16[1024,768]{1,0:T(8,128)(2,1)} %get-tuple-element.449), channel_id=1, source_target_pairs={{0,2},{2,4},{4,6},{6,8},{8,10},{10,12},{12,14},{14,16},{16,18},{18... | collective-permute-start | bytes 4718600 | tf_op jit(solution)/shard_map/while/body/eval_jaxpr/ppermute | solution.py:15
  142.4 21.8 %collective-permute-start.1 = (bf16[1024,768]{1,0:T(8,128)(2,1)}, bf16[1024,768]{1,0:T(8,128)(2,1)S(1)}, u32[]{:S(2)}, u32[]{:S(2)}) collective-permute-start(bf16[1024,768]{1,0:T(8,128)(2,1)} %get-tuple-element.450), channel_id=1, source_target_pairs={{2,0},{4,2},{6,4},{8,6},{10,8},{12,10},{14,12},{16,14},{18,16},{20... | collective-permute-start | bytes 4718600 | tf_op jit(solution)/shard_map/while/body/eval_jaxpr/ppermute | solution.py:15
  143.6 22.7 %collective-permute-start = (bf16[1024,768]{1,0:T(8,128)(2,1)}, bf16[1024,768]{1,0:T(8,128)(2,1)}, u32[]{:S(2)}, u32[]{:S(2)}) collective-permute-start(bf16[1024,768]{1,0:T(8,128)(2,1)} %get-tuple-element.449), channel_id=1, source_target_pairs={{0,2},{2,4},{4,6},{6,8},{8,10},{10,12},{12,14},{14,16},{16,18},{18... | collective-permute-start | bytes 4718600 | tf_op jit(solution)/shard_map/while/body/eval_jaxpr/ppermute | solution.py:15
  173.0 36.7 %collective-permute-start.1 = (bf16[1024,768]{1,0:T(8,128)(2,1)}, bf16[1024,768]{1,0:T(8,128)(2,1)S(1)}, u32[]{:S(2)}, u32[]{:S(2)}) collective-permute-start(bf16[1024,768]{1,0:T(8,128)(2,1)} %get-tuple-element.450), channel_id=1, source_target_pairs={{2,0},{4,2},{6,4},{8,6},{10,8},{12,10},{14,12},{16,14},{18,16},{20... | collective-permute-start | bytes 4718600 | tf_op jit(solution)/shard_map/while/body/eval_jaxpr/ppermute | solution.py:15
  174.3 37.6 %collective-permute-start = (bf16[1024,768]{1,0:T(8,128)(2,1)}, bf16[1024,768]{1,0:T(8,128)(2,1)}, u32[]{:S(2)}, u32[]{:S(2)}) collective-permute-start(bf16[1024,768]{1,0:T(8,128)(2,1)} %get-tuple-element.449), channel_id=1, source_target_pairs={{0,2},{2,4},{4,6},{6,8},{8,10},{10,12},{12,14},{14,16},{16,18},{18... | collective-permute-start | bytes 4718600 | tf_op jit(solution)/shard_map/while/body/eval_jaxpr/ppermute | solution.py:15
  310.4 21.7 %copy-start.2 = (bf16[16,64,6,64]{1,0,3,2:T(8,128)(2,1)S(1)}, bf16[16,64,6,64]{1,0,3,2:T(8,128)(2,1)}, u32[]{:S(2)}) copy-start(bf16[16,64,6,64]{1,0,3,2:T(8,128)(2,1)} %reshape.690) | copy-start | bytes 2359300
  345.4 11.9 copy-start.21
  357.3 16.7 %copy-start.23 = (f32[16,6,64]{2,1,0:T(8,128)}, f32[16,6,64]{2,1,0:T(8,128)S(1)}, u32[]{:S(2)}) copy-start(f32[16,6,64]{2,1,0:T(8,128)S(1)} %fusion.2) | copy-start | bytes 73732
  375.0 15.2 %copy-start.7 = (bf16[512,768]{1,0:T(8,128)(2,1)S(1)}, bf16[512,768]{1,0:T(8,128)(2,1)}, u32[]{:S(2)}) copy-start(bf16[512,768]{1,0:T(8,128)(2,1)} %param.19) | copy-start | bytes 2359300
  378.7 11.5 all-to-all-start.3
  391.1 24.4 %copy-start.11 = (f32[512,768]{1,0:T(8,128)}, f32[512,768]{1,0:T(8,128)S(1)}, u32[]{:S(2)}) copy-start(f32[512,768]{1,0:T(8,128)S(1)} %get-tuple-element.374) | copy-start | bytes 4718596
  391.1 24.4 %copy-start.25 = (f32[512]{0:T(512)}, f32[512]{0:T(512)S(1)}, u32[]{:S(2)}) copy-start(f32[512]{0:T(512)S(1)} %broadcast_multiply_fusion.5) | copy-start | bytes 6148
  391.5 24.1 %copy-start.35 = (f32[512]{0:T(512)}, f32[512]{0:T(512)S(1)}, u32[]{:S(2)}) copy-start(f32[512]{0:T(512)S(1)} %add_rsqrt_fusion.1) | copy-start | bytes 6148
  397.0 14.7 slice-start.2
  400.9 10.7 copy-start.10
  416.0 19.3 %copy-start.4 = (f32[512,768]{1,0:T(8,128)}, f32[512,768]{1,0:T(8,128)S(1)}, u32[]{:S(2)}) copy-start(f32[512,768]{1,0:T(8,128)S(1)} %subtract_multiply_fusion) | copy-start | bytes 4718596
  420.1 17.5 %all-to-all-start.4 = ((bf16[512,2,384]{0,2,1:T(8,128)(2,1)}), bf16[512,2,384]{0,2,1:T(8,128)(2,1)S(1)}, u32[]{:S(2)}, u32[]{:S(2)}) async-start(bf16[512,2,384]{0,2,1:T(8,128)(2,1)} %bitcast.289), calls=%async_computation.4 | async-start | bytes 1572864 | tf_op jit(solution)/shard_map/all_to_all | solution.py:204
  423.6 687.3 %reduce-scatter.13.cloned.1.call-start = ((), (), s32[]{:S(2)}) async-start(), calls=%async_computation.14 | async-start | bytes 2506752 | tf_op jit(solution)/shard_map/reduce_scatter | solution.py:288
  437.5 674.9 %reduce-scatter.23.cloned.1.call-start = ((), (), s32[]{:S(2)}) async-start(), calls=%async_computation.19 | async-start | bytes 2506752
  542.3 22.0 %copy-start.3 = (bf16[16,64,6,64]{1,0,3,2:T(8,128)(2,1)S(1)}, bf16[16,64,6,64]{1,0,3,2:T(8,128)(2,1)}, u32[]{:S(2)}) copy-start(bf16[16,64,6,64]{1,0,3,2:T(8,128)(2,1)} %reshape.690) | copy-start | bytes 2359300
  649.1 12.9 copy-start.62
  733.9 36.4 %collective-permute-start.2 = (bf16[1024,768]{1,0:T(8,128)(2,1)}, bf16[1024,768]{1,0:T(8,128)(2,1)}, u32[]{:S(2)}, u32[]{:S(2)}) collective-permute-start(bf16[1024,768]{1,0:T(8,128)(2,1)} %get-tuple-element.436), channel_id=1, source_target_pairs={{2,0},{4,2},{6,4},{8,6},{10,8},{12,10},{14,12},{16,14},{18,16},{20... | collective-permute-start | bytes 4718600 | tf_op jit(solution)/shard_map/while/body/eval_jaxpr/ppermute | solution.py:15
  735.2 38.5 %collective-permute-start.3 = (bf16[1024,768]{1,0:T(8,128)(2,1)S(1)}, bf16[1024,768]{1,0:T(8,128)(2,1)}, u32[]{:S(2)}, u32[]{:S(2)}) collective-permute-start(bf16[1024,768]{1,0:T(8,128)(2,1)S(1)} %get-tuple-element.437), channel_id=1, source_target_pairs={{0,2},{2,4},{4,6},{6,8},{8,10},{10,12},{12,14},{14,16},{16,18},{18... | collective-permute-start | bytes 4718600 | tf_op jit(solution)/shard_map/while/body/eval_jaxpr/ppermute | solution.py:15
  783.6 37.8 %collective-permute-start.2 = (bf16[1024,768]{1,0:T(8,128)(2,1)}, bf16[1024,768]{1,0:T(8,128)(2,1)}, u32[]{:S(2)}, u32[]{:S(2)}) collective-permute-start(bf16[1024,768]{1,0:T(8,128)(2,1)} %get-tuple-element.436), channel_id=1, source_target_pairs={{2,0},{4,2},{6,4},{8,6},{10,8},{12,10},{14,12},{16,14},{18,16},{20... | collective-permute-start | bytes 4718600 | tf_op jit(solution)/shard_map/while/body/eval_jaxpr/ppermute | solution.py:15
  784.9 39.8 %collective-permute-start.3 = (bf16[1024,768]{1,0:T(8,128)(2,1)S(1)}, bf16[1024,768]{1,0:T(8,128)(2,1)}, u32[]{:S(2)}, u32[]{:S(2)}) collective-permute-start(bf16[1024,768]{1,0:T(8,128)(2,1)S(1)} %get-tuple-element.437), channel_id=1, source_target_pairs={{0,2},{2,4},{4,6},{6,8},{8,10},{10,12},{12,14},{14,16},{16,18},{18... | collective-permute-start | bytes 4718600 | tf_op jit(solution)/shard_map/while/body/eval_jaxpr/ppermute | solution.py:15
  834.7 23.0 %collective-permute-start.2 = (bf16[1024,768]{1,0:T(8,128)(2,1)}, bf16[1024,768]{1,0:T(8,128)(2,1)}, u32[]{:S(2)}, u32[]{:S(2)}) collective-permute-start(bf16[1024,768]{1,0:T(8,128)(2,1)} %get-tuple-element.436), channel_id=1, source_target_pairs={{2,0},{4,2},{6,4},{8,6},{10,8},{12,10},{14,12},{16,14},{18,16},{20... | collective-permute-start | bytes 4718600 | tf_op jit(solution)/shard_map/while/body/eval_jaxpr/ppermute | solution.py:15
  836.0 25.1 %collective-permute-start.3 = (bf16[1024,768]{1,0:T(8,128)(2,1)S(1)}, bf16[1024,768]{1,0:T(8,128)(2,1)}, u32[]{:S(2)}, u32[]{:S(2)}) collective-permute-start(bf16[1024,768]{1,0:T(8,128)(2,1)S(1)} %get-tuple-element.437), channel_id=1, source_target_pairs={{0,2},{2,4},{4,6},{6,8},{8,10},{10,12},{12,14},{14,16},{16,18},{18... | collective-permute-start | bytes 4718600 | tf_op jit(solution)/shard_map/while/body/eval_jaxpr/ppermute | solution.py:15
  871.1 35.6 %collective-permute-start.2 = (bf16[1024,768]{1,0:T(8,128)(2,1)}, bf16[1024,768]{1,0:T(8,128)(2,1)}, u32[]{:S(2)}, u32[]{:S(2)}) collective-permute-start(bf16[1024,768]{1,0:T(8,128)(2,1)} %get-tuple-element.436), channel_id=1, source_target_pairs={{2,0},{4,2},{6,4},{8,6},{10,8},{12,10},{14,12},{16,14},{18,16},{20... | collective-permute-start | bytes 4718600 | tf_op jit(solution)/shard_map/while/body/eval_jaxpr/ppermute | solution.py:15
  872.4 37.6 %collective-permute-start.3 = (bf16[1024,768]{1,0:T(8,128)(2,1)S(1)}, bf16[1024,768]{1,0:T(8,128)(2,1)}, u32[]{:S(2)}, u32[]{:S(2)}) collective-permute-start(bf16[1024,768]{1,0:T(8,128)(2,1)S(1)} %get-tuple-element.437), channel_id=1, source_target_pairs={{0,2},{2,4},{4,6},{6,8},{8,10},{10,12},{12,14},{14,16},{16,18},{18... | collective-permute-start | bytes 4718600 | tf_op jit(solution)/shard_map/while/body/eval_jaxpr/ppermute | solution.py:15
  917.5 13.5 copy-start.8
  934.9 181.9 %reduce-scatter.21.cloned.1.call-start = ((), (), s32[]{:S(2)}) async-start(), calls=%async_computation.18 | async-start | bytes 2506752
  955.2 276.5 %reduce-scatter.17.cloned.1.call-start = ((), (), s32[]{:S(2)}) async-start(), calls=%async_computation.16 | async-start | bytes 10027008 | tf_op jit(solution)/shard_map/reduce_scatter | solution.py:292
  966.2 380.6 %reduce-scatter.15.cloned.1.call-start = ((), (), s32[]{:S(2)}) async-start(), calls=%async_computation.15 | async-start | bytes 10027008 | tf_op jit(solution)/shard_map/reduce_scatter | solution.py:291
  974.8 438.8 %reduce-scatter.19.cloned.1.call-start = ((), (), s32[]{:S(2)}) async-start(), calls=%async_computation.17 | async-start | bytes 2506752 | tf_op jit(solution)/shard_map/reduce_scatter | solution.py:285
  1001.6 347.0 %copy-start.17 = (bf16[2,512,384]{1,2,0:T(8,128)(2,1)S(1)}, bf16[2,512,384]{1,2,0:T(8,128)(2,1)}, u32[]{:S(2)}) copy-start(bf16[2,512,384]{1,2,0:T(8,128)(2,1)} %copy-done.16) | copy-start | bytes 2359300
  1001.6 347.0 %copy-start.63 = (bf16[768,768]{1,0:T(8,128)(2,1)S(1)}, bf16[768,768]{1,0:T(8,128)(2,1)}, u32[]{:S(2)}) copy-start(bf16[768,768]{1,0:T(8,128)(2,1)} %param.20) | copy-start | bytes 3538948
  1001.7 455.7 %all-reduce.10.cloned.1.call-start = ((), (), s32[]{:S(2)}) async-start(), calls=%async_computation.20 | async-start | bytes 2113536 | tf_op jit(solution)/shard_map/psum | solution.py:298
  1118.5 231.0 %copy-start.15 = (bf16[512,2,384]{0,2,1:T(8,128)(2,1)S(1)}, bf16[512,2,384]{0,2,1:T(8,128)(2,1)}, u32[]{:S(2)}) copy-start(bf16[512,2,384]{0,2,1:T(8,128)(2,1)} %copy.239) | copy-start | bytes 2359300
  1351.8 114.1 %copy-start.1 = (bf16[768,768]{1,0:T(8,128)(2,1)S(1)}, bf16[768,768]{1,0:T(8,128)(2,1)}, u32[]{:S(2)}) copy-start(bf16[768,768]{1,0:T(8,128)(2,1)} %param.23) | copy-start | bytes 3538948
  (55 other events, 276.6 us)
Sparse Core Ops, SparseCore 0:
  437.7 116.0 reduce-scatter.12
  935.0 115.9 reduce-scatter.22
  1054.7 62.0 reduce-scatter.20
  1121.3 110.3 reduce-scatter.16
  1235.6 111.0 reduce-scatter.14
  1350.9 62.7 reduce-scatter.18
  1417.4 39.9 all-reduce.9
